TPU v7x, 256 devices: a whole 4x4x8 slice. The times are simulated.
256 devices in a mesh: seq: 64 (over z, x, core), tensor: 4 (over y).
Axes of the slice: x: 4, y: 4, z: 8, core: 2. Of those that a mesh axis runs over, the one named last changes fastest.
Arguments:
- acts: bfloat16 [32768, 28672], P('seq', 'tensor'), may hold values from -6 to 6
- out_grads: bfloat16 [32768, 8192], P('seq', 'tensor'), may hold values from -6 to 6
- proj_in: bfloat16 [28672, 64], P('tensor'), may hold values from -0.03125 to 0.03125
- proj_out: bfloat16 [8192, 64], P('tensor'), may hold values from -0.0625 to 0.0625
- prior_cov: float32 [4096, 4096], P('seq', 'tensor'), may hold values from -0.2 to 0.2, as said below
Outputs:
- covariance: float32 [4096, 4096], P('seq', 'tensor')
Inputs may be any that keep to these rules, and one draw needn't show every extreme that they name: `prior_cov`: symmetric.
All inputs are finite; a program needn't handle non-finite values.
Results may differ from a plain program's by a relative error of at most 0.0003.
Values sent between devices are 32-bit elements; how exact they have to be, the bound alone decides.
A program may use at most 64 MiB of HBM per device.

v0:
```python
import jax
import jax.numpy as jnp
from jax import lax
from jax.sharding import PartitionSpec as P

RANK = 64
LEN = 256


def sent_to_all(value, axis):
    count = lax.axis_size(axis)
    return lax.all_to_all(
        jnp.broadcast_to(value[None], (count, *value.shape)), axis, 0, 0, tiled=True
    )


def of_everyone(value, axis):
    return sent_to_all(value, axis).sum(axis=0)


def laid_out(blocks, dim):
    blocks = jnp.moveaxis(blocks, 0, dim)
    shape = blocks.shape
    return blocks.reshape(*shape[:dim], shape[dim] * shape[dim + 1], *shape[dim + 2 :])


def gathered_copies(value, axis, dim):
    return laid_out(sent_to_all(value, axis), dim)


def example_grads(projected, seq_count):
    token_pos = jnp.arange(projected.shape[0], dtype=jnp.int32)
    owner = token_pos // LEN
    onehot = (owner[:, None] == jnp.arange(seq_count, dtype=jnp.int32)[None, :]).astype(jnp.float32)
    in_side = projected[:, :RANK]
    out_side = projected[:, RANK:]
    weighted = (onehot[:, :, None] * out_side[:, None, :]).reshape(
        projected.shape[0], seq_count * RANK
    )
    blocks = lax.dot_general(
        weighted, in_side, (((0,), (0,)), ((), ())), precision=lax.Precision.HIGHEST
    )
    return blocks.reshape(seq_count, RANK * RANK) / jnp.sqrt(jnp.float32(LEN))


def per_device(acts, out_grads, proj_in, proj_out, prior_cov):
    token_count = acts.shape[0]
    seq_count = token_count // LEN
    partial_value = jnp.concatenate(
        [
            jnp.dot(acts, proj_in, preferred_element_type=jnp.float32),
            jnp.dot(out_grads, proj_out, preferred_element_type=jnp.float32),
        ],
        axis=1,
    )
    summed = of_everyone(partial_value, "tensor")
    grads_ex = example_grads(summed, seq_count)
    col_width = prior_cov.shape[1]
    col_start = lax.axis_index("tensor") * col_width
    own_cols = lax.dynamic_slice_in_dim(grads_ex, col_start, col_width, 1)
    col_part = gathered_copies(own_cols, "seq", 0)
    row_part = lax.all_to_all(grads_ex, "seq", split_axis=1, concat_axis=0, tiled=True)
    total_seqs = col_part.shape[0]
    gram = lax.dot_general(
        row_part, col_part, (((0,), (0,)), ((), ())), precision=lax.Precision.HIGHEST
    )
    return prior_cov + gram / jnp.float32(total_seqs)


def solution(mesh):
    in_specs = (
        P("seq", "tensor"),
        P("seq", "tensor"),
        P("tensor", None),
        P("tensor", None),
        P("seq", "tensor"),
    )
    out_specs = P("seq", "tensor")
    return jax.shard_map(
        per_device, mesh=mesh, in_specs=in_specs, out_specs=out_specs, check_vma=False
    )
```

profile of v0, /device:TPU:1, one launch (start us, length us, event | category | flops | bytes accessed | tf_op | source)
XLA Modules:
  0.0 79.8 jit_solution(536458411463584621)
XLA Ops:
  0.0 0.0 copy-start
  0.0 1.6 %copy-done = bf16[512,2048]{1,0:T(8,128)(2,1)S(1)} copy-done((bf16[512,2048]{1,0:T(8,128)(2,1)S(1)}, bf16[512,2048]{1,0:T(8,128)(2,1)}, u32[]{:S(2)}) %copy-start) | copy-done | bytes 2097176
  1.6 1.7 %fusion.9 = f32[512,64]{0,1:T(8,128)S(1)} fusion(bf16[512,2048]{1,0:T(8,128)(2,1)S(1)} %copy-done, bf16[2048,64]{0,1:T(8,128)(2,1)} %param.8), kind=kOutput, calls=%fused_computation.19 | convolution fusion | flops 134217728 | bytes 2490368 | tf_op jit(solution)/shard_map/dot_general | solution.py:52
  3.3 5.6 %fusion.8 = f32[512,64]{0,1:T(8,128)S(1)} fusion(bf16[512,7168]{1,0:T(8,128)(2,1)} %param.5, bf16[7168,64]{0,1:T(8,128)(2,1)} %param.7), kind=kOutput, calls=%fused_computation.18 | convolution fusion | flops 469762048 | bytes 8388608 | tf_op jit(solution)/shard_map/dot_general | solution.py:51
  8.9 0.1 copy.16
  9.1 1.1 %broadcast_in_dim.4 = f32[4,512,128]{2,1,0:T(8,128)} broadcast(f32[512,128]{1,0:T(8,128)S(1)} %copy.16), dimensions={1,2} | broadcast | bytes 1310720 | tf_op jit(solution)/shard_map/broadcast_in_dim | solution.py:13
  10.1 5.0 %all-to-all-start = ((f32[4,512,128]{2,1,0:T(8,128)}), f32[4,512,128]{2,1,0:T(8,128)S(1)}, u32[]{:S(2)}, u32[]{:S(2)}) async-start(f32[4,512,128]{2,1,0:T(8,128)} %broadcast_in_dim.4), calls=%async_computation | async-start | bytes 2097152 | tf_op jit(solution)/shard_map/all_to_all | solution.py:12
  15.1 13.5 %all-to-all-done = f32[4,512,128]{2,1,0:T(8,128)S(1)} async-done(((f32[4,512,128]{2,1,0:T(8,128)}), f32[4,512,128]{2,1,0:T(8,128)S(1)}, u32[]{:S(2)}, u32[]{:S(2)}) %all-to-all-start) | async-done | bytes 1048608 | tf_op jit(solution)/shard_map/all_to_all | solution.py:12
  28.6 0.1 reduce_sum.9
  28.7 0.1 slice.8
  28.8 0.1 copy.17
  29.0 0.6 convolution_multiply_fusion
  29.6 0.1 copy.20
  29.7 0.1 div.28
  29.8 0.1 div.29
  29.9 0.1 copy.18
  30.0 0.7 reshape.52
  30.7 14.0 %all-to-all-start.1 = ((f32[64,1,128]{2,1,0:T(1,128)}), f32[64,1,128]{2,1,0:T(1,128)S(1)}, u32[]{:S(2)}, u32[]{:S(2)}) async-start(f32[64,1,128]{2,1,0:T(1,128)} %reshape.52), calls=%async_computation.1 | async-start | bytes 65536 | tf_op jit(solution)/shard_map/all_to_all | solution.py:62
  44.8 9.3 %all-to-all-done.1 = f32[64,1,128]{2,1,0:T(1,128)S(1)} async-done(((f32[64,1,128]{2,1,0:T(1,128)}), f32[64,1,128]{2,1,0:T(1,128)S(1)}, u32[]{:S(2)}, u32[]{:S(2)}) %all-to-all-start.1) | async-done | bytes 32800 | tf_op jit(solution)/shard_map/all_to_all | solution.py:62
  54.1 0.9 %broadcast_in_dim.5 = f32[64,2,1024]{2,1,0:T(2,128)} broadcast(f32[2,1024]{1,0:T(2,128)S(1)} %constant_dynamic-slice_fusion), dimensions={1,2} | broadcast | bytes 532480 | tf_op jit(solution)/shard_map/broadcast_in_dim | solution.py:13
  55.0 4.7 %all-to-all-start.2 = ((f32[64,2,1024]{2,1,0:T(2,128)}), f32[64,2,1024]{2,1,0:T(2,128)S(1)}, u32[]{:S(2)}, u32[]{:S(2)}) async-start(f32[64,2,1024]{2,1,0:T(2,128)} %broadcast_in_dim.5), calls=%async_computation.2 | async-start | bytes 1048576 | tf_op jit(solution)/shard_map/all_to_all | solution.py:12
  59.7 0.5 broadcast.54
  60.3 0.7 reduce
  61.0 0.1 reshape.53
  61.1 0.1 copy.19
  61.2 16.4 %all-to-all-done.2 = f32[64,2,1024]{2,1,0:T(2,128)S(1)} async-done(((f32[64,2,1024]{2,1,0:T(2,128)}), f32[64,2,1024]{2,1,0:T(2,128)S(1)}, u32[]{:S(2)}, u32[]{:S(2)}) %all-to-all-start.2) | async-done | bytes 524320 | tf_op jit(solution)/shard_map/all_to_all | solution.py:12
  77.5 2.2 %fusion.1 = f32[64,1024]{1,0:T(8,128)} fusion(f32[64,1024]{1,0:T(8,128)} %param.9, f32[64,2,1024]{2,1,0:T(2,128)S(1)} %all-to-all-done.2, f32[2,64,64]{1,2,0:T(8,128)S(1)} %copy.19), kind=kOutput, calls=%fused_computation.2 | convolution fusion | flops 100794368 | bytes 1081344 | tf_op jit(solution)/shard_map/dot_general | solution.py:64
  (5 shorter events, 0.1 us)
Async XLA Ops:
  0.0 1.6 %copy-start = (bf16[512,2048]{1,0:T(8,128)(2,1)S(1)}, bf16[512,2048]{1,0:T(8,128)(2,1)}, u32[]{:S(2)}) copy-start(bf16[512,2048]{1,0:T(8,128)(2,1)} %param.6) | copy-start | bytes 6291460
  10.1 18.5 %all-to-all-start = ((f32[4,512,128]{2,1,0:T(8,128)}), f32[4,512,128]{2,1,0:T(8,128)S(1)}, u32[]{:S(2)}, u32[]{:S(2)}) async-start(f32[4,512,128]{2,1,0:T(8,128)} %broadcast_in_dim.4), calls=%async_computation | async-start | bytes 2097152 | tf_op jit(solution)/shard_map/all_to_all | solution.py:12
  30.7 23.4 %all-to-all-start.1 = ((f32[64,1,128]{2,1,0:T(1,128)}), f32[64,1,128]{2,1,0:T(1,128)S(1)}, u32[]{:S(2)}, u32[]{:S(2)}) async-start(f32[64,1,128]{2,1,0:T(1,128)} %reshape.52), calls=%async_computation.1 | async-start | bytes 65536 | tf_op jit(solution)/shard_map/all_to_all | solution.py:62
  55.0 22.6 %all-to-all-start.2 = ((f32[64,2,1024]{2,1,0:T(2,128)}), f32[64,2,1024]{2,1,0:T(2,128)S(1)}, u32[]{:S(2)}, u32[]{:S(2)}) async-start(f32[64,2,1024]{2,1,0:T(2,128)} %broadcast_in_dim.5), calls=%async_computation.2 | async-start | bytes 1048576 | tf_op jit(solution)/shard_map/all_to_all | solution.py:12
where the time goes:
time: 80.1 us; the launch traced here: 79.8 us
  waiting for transfers between devices  39.2 us (49%)
  starting transfers between devices  23.8 us (30%)
  matrix products  10.1 us (13%)
  local copies, waits for them, and re-layouts  5.74 us (7%)
  other arithmetic  0.84 us (1%)
    all_to_all x2, waiting for transfers between devices, sent_to_all(): lax.all_to_all(jnp.broadcast_to(value[None], (count, *value.shape)), axis...  29.9 us
    all_to_all x1, starting transfers between devices, per_device(): lax.all_to_all(grads_ex, 'seq', split_axis=1, concat_axis=0, tiled=True)  14 us
    all_to_all x2, starting transfers between devices, sent_to_all(): lax.all_to_all(jnp.broadcast_to(value[None], (count, *value.shape)), axis...  9.74 us
    all_to_all x1, waiting for transfers between devices, per_device(): lax.all_to_all(grads_ex, 'seq', split_axis=1, concat_axis=0, tiled=True)  9.31 us
    dot_general x1, matrix products, per_device(): jnp.dot(acts, proj_in, preferred_element_type=jnp.float32)  5.61 us
    unnamed x4, local copies, waits for them, and re-layouts  2.42 us
    dot_general x1, matrix products, per_device(): lax.dot_general(row_part, col_part, (((0,), (0,)), ((), ())), precision=l...  2.21 us
    broadcast_in_dim x2, local copies, waits for them, and re-layouts, sent_to_all(): jnp.broadcast_to(value[None], (count, *value.shape))  1.97 us
  transfers between devices with their start and end apart: 3, of which 3 were waited for; matrix products, arithmetic and copies ran while one was open for 2% of the time, Pallas kernels for 0%

commit v1 on v0

v1 whole, which is shorter than its diff:
```python
import functools

import jax
import jax.numpy as jnp
from jax import lax
from jax.experimental import pallas as pl
from jax.experimental.pallas import tpu as pltpu
from jax.sharding import PartitionSpec as P

RANK = 64
LEN = 256
NZ, NX, NK, NC = 8, 4, 2, 4
MESH = pl.DeviceIdType.MESH
BF = jnp.bfloat16
F32 = jnp.float32
STOP = 9


def split(v):
    hi = v.astype(BF)
    return hi, (v - hi.astype(F32)).astype(BF)


def dot_t(a, b):
    return lax.dot_general(a, b, (((1,), (1,)), ((), ())), preferred_element_type=F32)


def dot(a, b):
    return lax.dot_general(a, b, (((1,), (0,)), ((), ())), preferred_element_type=F32)


def kernel(
    acts, grads, pin, pout, prior, out,
    a_v, g_v, pi_v, po_v, prior_v, part, rsbuf, tmp, pbuf, sbuf, rowl, rowz, rowt, rowbuf, colbuf,
    ld_sem, w_sem, rs_s, rs_r, p_s, p_r, z_s, z_r, zr_s, zr_r, x_s, x_r, c_s, c_r, r2_s, r2_r,
):
    r = lax.axis_index("seq")
    c = lax.axis_index("tensor")
    z = r // (NX * NK)
    x = (r // NK) % NX
    k = r % NK

    def seq_of(zz, xx, kk):
        return (zz * NX + xx) * NK + kk

    tok = acts.shape[0] // NC
    order = (2, 1, 3, 0)

    weights = [
        pltpu.make_async_copy(pin, pi_v, w_sem.at[0]),
        pltpu.make_async_copy(pout, po_v, w_sem.at[1]),
    ]
    prior_copy = pltpu.make_async_copy(prior, prior_v, w_sem.at[2])
    loads = []
    for n, dc in enumerate(order):
        rows = pl.ds(pl.multiple_of(((c + dc) % NC) * tok, tok), tok)
        loads.append(
            (
                pltpu.make_async_copy(acts.at[rows], a_v.at[n], ld_sem.at[n, 0]),
                pltpu.make_async_copy(grads.at[rows], g_v.at[n], ld_sem.at[n, 1]),
            )
        )
    weights[0].start()
    weights[1].start()
    for pair in loads:
        pair[0].start()
        pair[1].start()
    prior_copy.start()

    barrier = pltpu.get_barrier_semaphore()
    peers = [(r, (c + d) % NC) for d in range(1, NC)]
    peers += [(seq_of((z + d) % NZ, x, k), c) for d in range(1, NZ)]
    peers += [(seq_of(z, (x + d) % NX, kk), c) for d in range(1, NX) for kk in range(NK)]
    peers += [(seq_of(z, x, 1 - k), c)]
    for peer in peers:
        pl.semaphore_signal(barrier, inc=1, device_id=peer, device_id_type=MESH)

    def remote(src, dst, s, rs, peer):
        return pltpu.make_async_remote_copy(
            src_ref=src, dst_ref=dst, send_sem=s, recv_sem=rs, device_id=peer, device_id_type=MESH
        )

    weights[0].wait()
    weights[1].wait()
    sends = []
    for n, dc in enumerate(order):
        loads[n][0].wait()
        loads[n][1].wait()
        inp = dot_t(pi_v[...], a_v[n])
        outp = dot_t(po_v[...], g_v[n])
        if n == 0:
            pl.semaphore_wait(barrier, len(peers))
        if dc == 0:
            rsbuf[c, :RANK] = inp
            rsbuf[c, RANK:] = outp
        else:
            part[n, :RANK] = inp
            part[n, RANK:] = outp
            copy = remote(part.at[n], rsbuf.at[c], rs_s.at[dc], rs_r.at[dc], (r, (c + dc) % NC))
            copy.start()
            sends.append(copy)
    if STOP <= 1:
        for copy in sends:
            copy.wait()
        prior_copy.wait()
        out[...] = prior_v[...] + rsbuf[0, 0, 0]
        return
    for copy in sends:
        copy.wait_recv()
    both = (rsbuf[0] + rsbuf[1]) + (rsbuf[2] + rsbuf[3])
    hi, lo = split(both)
    in_hi, in_lo = hi[:RANK], lo[:RANK]
    o_hi, o_lo = hi[RANK:], lo[RANK:]
    dup_hi = jnp.concatenate([in_hi, in_hi], axis=0)
    dup_lo = jnp.concatenate([in_lo, in_lo], axis=0)
    tmp[...] = dot_t(o_hi, dup_hi) + (dot_t(o_hi, dup_lo) + dot_t(o_lo, dup_hi))
    half = RANK // 2
    low = lax.broadcasted_iota(jnp.int32, (half, 2 * RANK), 1) < RANK
    pbuf[c] = jnp.where(low, tmp[pl.ds(0, half, stride=2), :], tmp[pl.ds(1, half, stride=2), :])

    p_copies = []
    for dc in (2, 1, 3):
        copy = remote(pbuf.at[c], pbuf.at[c], p_s.at[dc], p_r.at[dc], (r, (c + dc) % NC))
        copy.start()
        p_copies.append(copy)
    for copy in p_copies:
        copy.wait_recv()
    scale = 1.0 / 16.0
    s0 = (pbuf[0] + pbuf[1]) * scale
    s1 = (pbuf[2] + pbuf[3]) * scale
    sbuf[:half] = s0
    sbuf[half:] = s1
    rowl[pl.ds(0, half, stride=2), :] = jnp.where(low, s0, pltpu.roll(s1, RANK, 1))
    rowl[pl.ds(1, half, stride=2), :] = jnp.where(low, pltpu.roll(s0, RANK, 1), s1)

    def piece(xx, kk, zz):
        return pl.ds(pl.multiple_of(((xx * NK + kk) * NZ + zz) * 16, 16), 16)

    def tile(i):
        return pl.ds(pl.multiple_of(i * 8, 8), 8)

    own = pl.multiple_of(((x * NK + k) * NZ + z) * 16, 16)
    colbuf[pl.ds(own, 8), :] = sbuf[tile(c), :]
    colbuf[pl.ds(own + 8, 8), :] = sbuf[tile(c + NC), :]
    rowz[tile(z), :] = rowl[tile(z), :]
    if STOP <= 2:
        for copy in sends + p_copies:
            copy.wait_send()
        prior_copy.wait()
        out[...] = prior_v[...] + colbuf[0, 0]
        return

    def z_col(dz):
        ref = colbuf.at[piece(x, k, z)]
        return remote(ref, ref, z_s, z_r.at[dz], (seq_of((z + dz) % NZ, x, k), c))

    def z_row(dz):
        zz = (z + dz) % NZ
        return remote(rowl.at[tile(zz)], rowz.at[tile(z)], zr_s, zr_r, (seq_of(zz, x, k), c))

    def x_col(dx, dz):
        ref = colbuf.at[piece(x, k, (z - dz) % NZ)]
        return remote(ref, ref, x_s, x_r.at[dx, dz], (seq_of(z, (x + dx) % NX, k), c))

    def c_col(dx, dz):
        ref = colbuf.at[piece((x - dx) % NX, k, (z - dz) % NZ)]
        return remote(ref, ref, c_s, c_r, (seq_of(z, x, 1 - k), c))

    for dz in (4, 3, 5, 2, 6, 1, 7):
        z_row(dz).start()
        z_col(dz).start()

    def have_z(dz):
        if dz:
            z_col(dz).wait_recv()
        for dx in (2, 1, 3):
            x_col(dx, dz).start()
        c_col(0, dz).start()

    def have_x(dx, dz):
        x_col(dx, dz).wait_recv()
        c_col(dx, dz).start()

    have_z(0)
    for dz in (1, 7):
        have_z(dz)
    for dz in (2, 6):
        have_z(dz)
    for dx in (1, 3, 2):
        have_x(dx, 0)
    for dz in (3, 5):
        have_z(dz)
    for dx in (1, 3):
        for dz in (1, 7):
            have_x(dx, dz)
    have_z(4)

    pltpu.make_async_copy(rowz.at[pl.ds(0, 56)], rowz.at[pl.ds(0, 56)], zr_r).wait()
    for j in range(8):
        rowt[8 * j : 8 * j + 8, :] = rowz[pl.ds(j, 8, stride=8), :]
    me = x * NK + k
    rowbuf[tile(me), :] = rowt[tile(me), :]
    for dx in (2, 1, 3, 0):
        for dk in range(NK):
            if dx or dk:
                xx = (x + dx) % NX
                kk = (k + dk) % NK
                remote(
                    rowt.at[tile(xx * NK + kk)], rowbuf.at[tile(me)], r2_s, r2_r, (seq_of(z, xx, kk), c)
                ).start()

    for dz in (1, 7):
        have_x(2, dz)
    for dz in (2, 6, 3, 5, 4):
        for dx in (1, 3, 2):
            have_x(dx, dz)

    pltpu.make_async_copy(rowbuf.at[pl.ds(0, 56)], rowbuf.at[pl.ds(0, 56)], r2_r).wait()
    flipped = rowbuf[...].T
    lhs = jnp.concatenate([flipped[:RANK], flipped[RANK:]], axis=1)
    l_hi, l_lo = split(lhs)
    pltpu.make_async_copy(colbuf.at[pl.ds(0, 512)], colbuf.at[pl.ds(0, 512)], c_r).wait()
    prior_copy.wait()
    for p in range(8):
        block = jnp.concatenate(
            [colbuf[pl.ds(p, 64, stride=16), :], colbuf[pl.ds(8 + p, 64, stride=16), :]], axis=0
        )
        b_hi, b_lo = split(block)
        gram = dot(l_hi, b_hi) + (dot(l_hi, b_lo) + dot(l_lo, b_hi))
        cols = slice(128 * p, 128 * p + 128)
        out[:, cols] = prior_v[:, cols] + gram * (1.0 / 128.0)

    for copy in sends + p_copies:
        copy.wait_send()
    here = (r, c)
    for sem, rows in ((z_s, 112), (x_s, 384), (c_s, 512)):
        ref = colbuf.at[pl.ds(0, rows)]
        pltpu.make_async_copy(ref, ref, sem).wait()
    for sem in (zr_s, r2_s):
        pltpu.make_async_copy(rowz.at[pl.ds(0, 56)], rowz.at[pl.ds(0, 56)], sem).wait()


def per_device(acts, out_grads, proj_in, proj_out, prior_cov):
    tokens, ff = acts.shape
    d = out_grads.shape[1]
    tok = tokens // NC
    hbm = pl.BlockSpec(memory_space=pl.ANY)
    dma = pltpu.SemaphoreType.DMA
    return pl.pallas_call(
        kernel,
        out_shape=jax.ShapeDtypeStruct(prior_cov.shape, F32),
        in_specs=[hbm] * 5,
        out_specs=pl.BlockSpec(memory_space=pltpu.VMEM),
        scratch_shapes=[
            pltpu.VMEM((NC, tok, ff), BF),
            pltpu.VMEM((NC, tok, d), BF),
            pltpu.VMEM((RANK, ff), BF),
            pltpu.VMEM((RANK, d), BF),
            pltpu.VMEM(prior_cov.shape, F32),
            pltpu.VMEM((3, 2 * RANK, tok), F32),
            pltpu.VMEM((NC, 2 * RANK, tok), F32),
            pltpu.VMEM((RANK, 2 * RANK), F32),
            pltpu.VMEM((NC, RANK // 2, 2 * RANK), F32),
            pltpu.VMEM((RANK, 2 * RANK), F32),
            pltpu.VMEM((RANK, 2 * RANK), F32),
            pltpu.VMEM((RANK, 2 * RANK), F32),
            pltpu.VMEM((RANK, 2 * RANK), F32),
            pltpu.VMEM((RANK, 2 * RANK), F32),
            pltpu.VMEM((RANK * 16, 2 * RANK), F32),
            dma((NC, 2)),
            dma((3,)),
            dma((NC,)),
            dma((NC,)),
            dma((NC,)),
            dma((NC,)),
            dma(()),
            dma((NZ,)),
            dma(()),
            dma(()),
            dma(()),
            dma((NX, NZ)),
            dma(()),
            dma(()),
            dma(()),
            dma(()),
        ],
        compiler_params=pltpu.CompilerParams(
            collective_id=0, has_side_effects=True, vmem_limit_bytes=56 * 1024 * 1024
        ),
    )(acts, out_grads, proj_in.T, proj_out.T, prior_cov)


def solution(mesh):
    in_specs = (
        P("seq", "tensor"),
        P("seq", "tensor"),
        P("tensor", None),
        P("tensor", None),
        P("seq", "tensor"),
    )
    return jax.shard_map(
        per_device, mesh=mesh, in_specs=in_specs, out_specs=P("seq", "tensor"), check_vma=False
    )
```

time: 80.1 us -> 36.8 us (0.46)
  waiting for transfers between devices: 39.2 us -> 0 us
  Pallas kernels: 0 us -> 35 us
  starting transfers between devices: 23.8 us -> 0 us
  matrix products: 10.1 us -> 0 us
  local copies, waits for them, and re-layouts: 5.74 us -> 1.67 us
  other arithmetic: 0.84 us -> 0 us
    all_to_all x3 -> x0, waiting for transfers between devices: 39.2 us -> none  [the longest x2 29.9 us: sent_to_all(): lax.all_to_all(jnp.broadcast_to(value[None], (count, *value.shape)), axis...]
    pallas_call x0 -> x1, Pallas kernels: none -> 35 us  [per_device(): pl.pallas_call(kernel, out_shape=jax.ShapeDtypeStruct(prior_cov.shape, F3...]
    all_to_all x3 -> x0, starting transfers between devices: 23.8 us -> none  [the longest x1 14 us: per_device(): lax.all_to_all(grads_ex, 'seq', split_axis=1, concat_axis=0, tiled=True)]
    dot_general x4 -> x0, matrix products: 10.1 us -> none  [the longest x1 5.61 us: per_device(): jnp.dot(acts, proj_in, preferred_element_type=jnp.float32)]
    broadcast_in_dim x2 -> x0, local copies, waits for them, and re-layouts: 1.97 us -> none  [sent_to_all(): jnp.broadcast_to(value[None], (count, *value.shape))]
    unnamed x4 -> x1, local copies, waits for them, and re-layouts: 2.42 us -> 1.67 us
  transfers between devices with their start and end apart: 3 -> 0, of which waited for: 3 -> 0; matrix products, arithmetic and copies ran while one was open for 2% -> 0% of each run, Pallas kernels for 0% -> 0%
where the time goes in v1:
time: 36.8 us; the launch traced here: 36.7 us
  Pallas kernels  35 us (95%)
  local copies, waits for them, and re-layouts  1.67 us (5%)
    pallas_call x1, Pallas kernels, per_device(): pl.pallas_call(kernel, out_shape=jax.ShapeDtypeStruct(prior_cov.shape, F3...  35 us
    unnamed x1, local copies, waits for them, and re-layouts  1.67 us

profile of v1, /device:TPU:1, one launch (start us, length us, event | category | flops | bytes accessed | tf_op | source)
XLA Modules:
  0.0 36.7 jit_solution(8534347597563199757)
XLA Ops:
  0.0 35.0 %shard_map.55 = f32[64,1024]{1,0:T(8,128)} custom-call(bf16[512,7168]{1,0:T(8,128)(2,1)} %acts.1, bf16[512,2048]{1,0:T(8,128)(2,1)} %grads.1, bf16[64,7168]{1,0:T(8,128)(2,1)} %bitcast.2, bf16[64,2048]{1,0:T(8,128)(2,1)} %bitcast.3, f32[64,1024]{1,0:T(8,128)} %prior.1), custom_call_target="tpu_custom_call" | custom-call | tf_op jit(solution)/shard_map/pallas_call | solution.py:249
  35.0 1.7 %copy.7 = f32[64,1024]{1,0:T(8,128)} copy(f32[64,1024]{1,0:T(8,128)} %shard_map.55) | data formatting | bytes 524288

commit v2 on v1

v2 whole, which is shorter than its diff:
```python
import functools

import jax
import jax.numpy as jnp
from jax import lax
from jax.experimental import pallas as pl
from jax.experimental.pallas import tpu as pltpu
from jax.sharding import PartitionSpec as P

RANK = 64
LEN = 256
NZ, NX, NK, NC = 8, 4, 2, 4
MESH = pl.DeviceIdType.MESH
BF = jnp.bfloat16
F32 = jnp.float32
STOP = 9
CUTS = 1
GROUPS = (2, 1, 3, 0)
MEET = 0
WINDOW = 3


def split(v):
    hi = v.astype(BF)
    return hi, (v - hi.astype(F32)).astype(BF)


def dot_t(a, b):
    return lax.dot_general(a, b, (((1,), (1,)), ((), ())), preferred_element_type=F32)


def dot(a, b):
    return lax.dot_general(a, b, (((1,), (0,)), ((), ())), preferred_element_type=F32)


def kernel(
    acts, grads, pin, pout, prior, out,
    a_v, g_v, pi_v, po_v, prior_v, part, rsbuf, tmp, pbuf, sbuf, rowl, rowbuf, colbuf,
    ld_sem, w_sem, rs_s, rs_r, p_s, p_r, col_s, col_r, row_s, row_r, cc_s, cc_r, cr_s, cr_r, met,
):
    r = lax.axis_index("seq")
    c = lax.axis_index("tensor")
    z = r // (NX * NK)
    x = (r // NK) % NX
    k = r % NK

    def seq_of(zz, xx, kk):
        return (zz * NX + xx) * NK + kk

    tok = acts.shape[0] // NC
    ff = acts.shape[1]
    wide = ff // CUTS
    order = (2, 1, 3, 0)

    weights = [
        pltpu.make_async_copy(pin, pi_v, w_sem.at[0]),
        pltpu.make_async_copy(pout, po_v, w_sem.at[1]),
    ]
    prior_copy = pltpu.make_async_copy(prior, prior_v, w_sem.at[2])
    loads = []
    for n, dc in enumerate(order):
        rows = pl.ds(pl.multiple_of(((c + dc) % NC) * tok, tok), tok)
        for cut in range(CUTS):
            cols = pl.ds(cut * wide, wide)
            loads.append(
                pltpu.make_async_copy(acts.at[rows, cols], a_v.at[n, :, cols], ld_sem.at[n, cut])
            )
        loads.append(pltpu.make_async_copy(grads.at[rows], g_v.at[n], ld_sem.at[n, CUTS]))
    weights[0].start()
    for load in loads[:CUTS]:
        load.start()
    weights[1].start()
    for load in loads[CUTS:WINDOW]:
        load.start()

    barrier = pltpu.get_barrier_semaphore()
    peers = [(r, (c + d) % NC) for d in range(1, NC)]
    peers += [(seq_of(z, x, 1 - k), c)]
    line = {d: (seq_of((z + d) % NZ, x, k), c) for d in (1, 2, NZ - 2, NZ - 1)}
    across = [(seq_of(z, (x + d) % NX, k), c) for d in range(1, NX)]
    peers += [line[1], line[NZ - 1]] + across

    def tell(sem, group):
        for peer in group:
            pl.semaphore_signal(sem, inc=1, device_id=peer, device_id_type=MESH)

    tell(barrier, peers)

    def remote(src, dst, s, rs, peer):
        return pltpu.make_async_remote_copy(
            src_ref=src, dst_ref=dst, send_sem=s, recv_sem=rs, device_id=peer, device_id_type=MESH
        )

    pending = iter(loads[WINDOW:] + [prior_copy])

    def arrived(load):
        load.wait()
        follower = next(pending, None)
        if follower is not None:
            follower.start()

    sends = []
    weights[0].wait()
    for n, dc in enumerate(order):
        inp = None
        for cut in range(CUTS):
            arrived(loads[n * (CUTS + 1) + cut])
            cols = slice(cut * wide, cut * wide + wide)
            term = dot_t(a_v[n, :, cols], pi_v[:, cols])
            inp = term if inp is None else inp + term
        arrived(loads[n * (CUTS + 1) + CUTS])
        if n == 0:
            weights[1].wait()
        outp = dot_t(g_v[n], po_v[...])
        if dc == 0:
            rsbuf[c, :, :RANK] = inp
            rsbuf[c, :, RANK:] = outp
        else:
            part[n, :, :RANK] = inp
            part[n, :, RANK:] = outp
        if n == MEET:
            pl.semaphore_wait(barrier, len(peers))
            tell(met.at[0], [line[1], line[NZ - 1]])
        if n >= MEET:
            for m in range(0 if n == MEET else n, n + 1):
                dm = order[m]
                if dm and STOP > 0:
                    peer = (r, (c + dm) % NC)
                    copy = remote(part.at[m], rsbuf.at[c], rs_s.at[dm], rs_r.at[dm], peer)
                    copy.start()
                    sends.append(copy)
    pl.semaphore_wait(met.at[0], 2)
    tell(met.at[1], [line[2], line[NZ - 2]])
    if STOP <= 1:
        for copy in sends:
            copy.wait()
        prior_copy.wait()
        pl.semaphore_wait(met.at[1], 2)
        out[...] = prior_v[...] + rsbuf[0, 0, 0]
        return
    for copy in sends:
        copy.wait_recv()
    both = ((rsbuf[0] + rsbuf[1]) + (rsbuf[2] + rsbuf[3])).T
    hi, lo = split(both)
    in_hi, in_lo = hi[:RANK], lo[:RANK]
    o_hi, o_lo = hi[RANK:], lo[RANK:]
    dup_hi = jnp.concatenate([in_hi, in_hi], axis=0)
    dup_lo = jnp.concatenate([in_lo, in_lo], axis=0)
    tmp[...] = dot_t(o_hi, dup_hi) + (dot_t(o_hi, dup_lo) + dot_t(o_lo, dup_hi))
    half = RANK // 2
    low = lax.broadcasted_iota(jnp.int32, (half, 2 * RANK), 1) < RANK
    pbuf[c] = jnp.where(low, tmp[pl.ds(0, half, stride=2), :], tmp[pl.ds(1, half, stride=2), :])

    p_copies = []
    for dc in (2, 1, 3):
        copy = remote(pbuf.at[c], pbuf.at[c], p_s.at[dc], p_r.at[dc], (r, (c + dc) % NC))
        copy.start()
        p_copies.append(copy)
    pl.semaphore_wait(met.at[1], 2)
    tell(met.at[2], across)
    for copy in p_copies:
        copy.wait_recv()
    pl.semaphore_wait(met.at[2], NX - 1)
    scale = 1.0 / 16.0
    s0 = (pbuf[0] + pbuf[1]) * scale
    s1 = (pbuf[2] + pbuf[3]) * scale
    sbuf[:half] = s0
    sbuf[half:] = s1
    rowl[:, 0, :] = s0
    rowl[:, 1, :] = s1

    def slot(zz, xx, kk):
        return (kk * NX + xx) * NZ + zz

    def piece(i):
        return colbuf.at[pl.ds(pl.multiple_of(i * 16, 16), 16)]

    def tile(i):
        return pl.ds(pl.multiple_of(i * 8, 8), 8)

    me = slot(z, x, k)
    own = pl.multiple_of(me * 16, 16)
    colbuf[pl.ds(own, 8), :] = sbuf[tile(c), :]
    colbuf[pl.ds(own + 8, 8), :] = sbuf[tile(c + NC), :]
    rowbuf[me] = rowl[z * NX + x]
    if STOP <= 2:
        for copy in sends + p_copies:
            copy.wait_send()
        prior_copy.wait()
        out[...] = prior_v[...] + colbuf[0, 0]
        return

    def col(dz, dx):
        peer = (seq_of((z + dz) % NZ, (x + dx) % NX, k), c)
        return remote(piece(me), piece(me), col_s, col_r.at[dx], peer)

    def row(dz, dx):
        zz, xx = (z + dz) % NZ, (x + dx) % NX
        return remote(rowl.at[zz * NX + xx], rowbuf.at[me], row_s, row_r.at[dx], (seq_of(zz, xx, k), c))

    sibling = (seq_of(z, x, 1 - k), c)

    def col_group(xx, count):
        return colbuf.at[pl.ds(pl.multiple_of(slot(0, xx, k) * 16, 128), count * 16)]

    def row_group(xx, count):
        return rowbuf.at[pl.ds(slot(0, xx, k), count)]

    for dx in GROUPS:
        for dz in (4, 3, 5, 2, 6, 1, 7, 0):
            if dz or dx:
                row(dz, dx).start()
                col(dz, dx).start()
    for dx in GROUPS:
        count = NZ if dx else NZ - 1
        xx = (x - dx) % NX
        for group, arrival, s, rs in ((col_group, col_r, cc_s, cc_r), (row_group, row_r, cr_s, cr_r)):
            got = group(xx, count)
            pltpu.make_async_copy(got, got, arrival.at[dx]).wait()
            whole = group(xx, NZ)
            remote(whole, whole, s, rs, sibling).start()

    total = NZ * NX
    mine = colbuf.at[pl.ds(0, total * 16)]
    mine_rows = rowbuf.at[pl.ds(0, total)]
    pltpu.make_async_copy(mine_rows, mine_rows, cr_r).wait()
    even = (jnp.zeros((NZ * NX * NK, 2 * RANK), jnp.int32) + k) == 0
    parts = []
    for h in range(2):
        v = rowbuf[:, h, :]
        parts.append(jnp.where(even, v, pltpu.roll(v, RANK, 1)))
    lhs = jnp.concatenate(parts, axis=0).T[:RANK]
    l_hi, l_lo = split(lhs)
    prior_copy.wait()
    pltpu.make_async_copy(mine, mine, cc_r).wait()
    for p in range(8):
        block = jnp.concatenate(
            [colbuf[pl.ds(p, 64, stride=16), :], colbuf[pl.ds(8 + p, 64, stride=16), :]], axis=0
        )
        b_hi, b_lo = split(block)
        gram = dot(l_hi, b_hi) + (dot(l_hi, b_lo) + dot(l_lo, b_hi))
        cols = slice(128 * p, 128 * p + 128)
        out[:, cols] = prior_v[:, cols] + gram * (1.0 / 128.0)

    for copy in sends + p_copies:
        copy.wait_send()
    others = colbuf.at[pl.ds(0, (total - 1) * 16)]
    other_rows = rowbuf.at[pl.ds(0, total - 1)]
    pltpu.make_async_copy(others, others, col_s).wait()
    pltpu.make_async_copy(other_rows, other_rows, row_s).wait()
    pltpu.make_async_copy(mine, mine, cc_s).wait()
    pltpu.make_async_copy(mine_rows, mine_rows, cr_s).wait()


def per_device(acts, out_grads, proj_in, proj_out, prior_cov):
    tokens, ff = acts.shape
    d = out_grads.shape[1]
    tok = tokens // NC
    hbm = pl.BlockSpec(memory_space=pl.ANY)
    dma = pltpu.SemaphoreType.DMA
    return pl.pallas_call(
        kernel,
        out_shape=pltpu.VMEM(prior_cov.shape, F32),
        in_specs=[hbm] * 5,
        out_specs=pl.BlockSpec(memory_space=pltpu.VMEM),
        scratch_shapes=[
            pltpu.VMEM((NC, tok, ff), BF),
            pltpu.VMEM((NC, tok, d), BF),
            pltpu.VMEM((RANK, ff), BF),
            pltpu.VMEM((RANK, d), BF),
            pltpu.VMEM(prior_cov.shape, F32),
            pltpu.VMEM((3, tok, 2 * RANK), F32),
            pltpu.VMEM((NC, tok, 2 * RANK), F32),
            pltpu.VMEM((RANK, 2 * RANK), F32),
            pltpu.VMEM((NC, RANK // 2, 2 * RANK), F32),
            pltpu.VMEM((RANK, 2 * RANK), F32),
            pltpu.VMEM((RANK // 2, 2, 2 * RANK), F32),
            pltpu.VMEM((RANK, 2, 2 * RANK), F32),
            pltpu.VMEM((RANK * 16, 2 * RANK), F32),
            dma((NC, CUTS + 1)),
            dma((3,)),
            dma((NC,)),
            dma((NC,)),
            dma((NC,)),
            dma((NC,)),
            dma(()),
            dma((NX,)),
            dma(()),
            dma((NX,)),
            dma(()),
            dma(()),
            dma(()),
            dma(()),
            pltpu.SemaphoreType.REGULAR((3,)),
        ],
        compiler_params=pltpu.CompilerParams(
            collective_id=0, has_side_effects=True, vmem_limit_bytes=56 * 1024 * 1024
        ),
    )(acts, out_grads, proj_in.T, proj_out.T, prior_cov)


def solution(mesh):
    in_specs = (
        P("seq", "tensor"),
        P("seq", "tensor"),
        P("tensor", None),
        P("tensor", None),
        P("seq", "tensor"),
    )
    return jax.shard_map(
        per_device, mesh=mesh, in_specs=in_specs, out_specs=P("seq", "tensor"), check_vma=False
    )
```

time: 36.8 us -> 31.6 us (0.86)
  Pallas kernels: 35 us -> 30.8 us
  local copies, waits for them, and re-layouts: 1.67 us -> 0.71 us
    pallas_call x1, Pallas kernels: 35 us -> 30.8 us  [per_device(): pl.pallas_call(kernel, out_shape=pltpu.VMEM(prior_cov.shape, F32), in_spe...]
    unnamed x1, local copies, waits for them, and re-layouts: 1.67 us -> 0.71 us
where the time goes in v2:
time: 31.6 us; the launch traced here: 31.5 us
  Pallas kernels  30.8 us (97%)
  local copies, waits for them, and re-layouts  0.71 us (2%)
    pallas_call x1, Pallas kernels, per_device(): pl.pallas_call(kernel, out_shape=pltpu.VMEM(prior_cov.shape, F32), in_spe...  30.8 us
    unnamed x1, local copies, waits for them, and re-layouts  0.71 us

profile of v2, /device:TPU:1, one launch (start us, length us, event | category | flops | bytes accessed | tf_op | source)
XLA Modules:
  0.0 31.5 jit_solution(16964067282762581002)
XLA Ops:
  0.0 30.8 %shard_map.55 = f32[64,1024]{1,0:T(8,128)S(1)} custom-call(bf16[512,7168]{1,0:T(8,128)(2,1)} %acts.1, bf16[512,2048]{1,0:T(8,128)(2,1)} %grads.1, bf16[64,7168]{1,0:T(8,128)(2,1)} %bitcast.2, bf16[64,2048]{1,0:T(8,128)(2,1)} %bitcast.3, f32[64,1024]{1,0:T(8,128)} %prior.1), custom_call_target="tpu_custom_call" | custom-call | tf_op jit(solution)/shard_map/pallas_call | solution.py:261
  30.8 0.7 %copy.7 = f32[64,1024]{1,0:T(8,128)} copy(f32[64,1024]{1,0:T(8,128)S(1)} %shard_map.55) | data formatting | bytes 524288

commit v3 on v2

--- a/solution.py
+++ b/solution.py
@@ -14,10 +14,7 @@
 BF = jnp.bfloat16
 F32 = jnp.float32
 STOP = 9
-CUTS = 1
 GROUPS = (2, 1, 3, 0)
-MEET = 0
-WINDOW = 3
 
 
 def split(v):
@@ -48,30 +45,29 @@
         return (zz * NX + xx) * NK + kk
 
     tok = acts.shape[0] // NC
-    ff = acts.shape[1]
-    wide = ff // CUTS
-    order = (2, 1, 3, 0)
-
     weights = [
         pltpu.make_async_copy(pin, pi_v, w_sem.at[0]),
         pltpu.make_async_copy(pout, po_v, w_sem.at[1]),
     ]
     prior_copy = pltpu.make_async_copy(prior, prior_v, w_sem.at[2])
-    loads = []
-    for n, dc in enumerate(order):
-        rows = pl.ds(pl.multiple_of(((c + dc) % NC) * tok, tok), tok)
-        for cut in range(CUTS):
-            cols = pl.ds(cut * wide, wide)
-            loads.append(
-                pltpu.make_async_copy(acts.at[rows, cols], a_v.at[n, :, cols], ld_sem.at[n, cut])
-            )
-        loads.append(pltpu.make_async_copy(grads.at[rows], g_v.at[n], ld_sem.at[n, CUTS]))
+
+    def shift(n):
+        return (2 + 3 * n + 3 * (n * (n - 1) // 2)) % NC
+
+    def rows_of(n):
+        return pl.ds(pl.multiple_of(((c + shift(n)) % NC) * tok, tok), tok)
+
+    def load_acts(n):
+        return pltpu.make_async_copy(acts.at[rows_of(n)], a_v.at[n], ld_sem.at[n, 0])
+
+    def load_grads(n):
+        return pltpu.make_async_copy(grads.at[rows_of(n)], g_v.at[n], ld_sem.at[n, 1])
+
     weights[0].start()
-    for load in loads[:CUTS]:
-        load.start()
+    load_acts(0).start()
     weights[1].start()
-    for load in loads[CUTS:WINDOW]:
-        load.start()
+    load_grads(0).start()
+    load_acts(1).start()
 
     barrier = pltpu.get_barrier_semaphore()
     peers = [(r, (c + d) % NC) for d in range(1, NC)]
@@ -91,44 +87,49 @@
             src_ref=src, dst_ref=dst, send_sem=s, recv_sem=rs, device_id=peer, device_id_type=MESH
         )
 
-    pending = iter(loads[WINDOW:] + [prior_copy])
-
-    def arrived(load):
-        load.wait()
-        follower = next(pending, None)
-        if follower is not None:
-            follower.start()
-
-    sends = []
+    def rs_copy(n):
+        dc = shift(n)
+        peer = (r, (c + dc) % NC)
+        return remote(part.at[n], rsbuf.at[dc], rs_s.at[dc], rs_r.at[dc], peer)
+
     weights[0].wait()
-    for n, dc in enumerate(order):
-        inp = None
-        for cut in range(CUTS):
-            arrived(loads[n * (CUTS + 1) + cut])
-            cols = slice(cut * wide, cut * wide + wide)
-            term = dot_t(a_v[n, :, cols], pi_v[:, cols])
-            inp = term if inp is None else inp + term
-        arrived(loads[n * (CUTS + 1) + CUTS])
-        if n == 0:
-            weights[1].wait()
-        outp = dot_t(g_v[n], po_v[...])
-        if dc == 0:
-            rsbuf[c, :, :RANK] = inp
-            rsbuf[c, :, RANK:] = outp
-        else:
-            part[n, :, :RANK] = inp
-            part[n, :, RANK:] = outp
-        if n == MEET:
+    weights[1].wait()
+
+    def block(n, carry):
+        load_acts(n).wait()
+
+        @pl.when(n < NC - 1)
+        def _():
+            load_grads(n + 1).start()
+
+        part[n, :, :RANK] = dot_t(a_v[n], pi_v[...])
+        load_grads(n).wait()
+
+        @pl.when(n < NC - 2)
+        def _():
+            load_acts(n + 2).start()
+
+        @pl.when(n == NC - 2)
+        def _():
+            prior_copy.start()
+
+        part[n, :, RANK:] = dot_t(g_v[n], po_v[...])
+
+        @pl.when(n == 0)
+        def _():
             pl.semaphore_wait(barrier, len(peers))
             tell(met.at[0], [line[1], line[NZ - 1]])
-        if n >= MEET:
-            for m in range(0 if n == MEET else n, n + 1):
-                dm = order[m]
-                if dm and STOP > 0:
-                    peer = (r, (c + dm) % NC)
-                    copy = remote(part.at[m], rsbuf.at[c], rs_s.at[dm], rs_r.at[dm], peer)
-                    copy.start()
-                    sends.append(copy)
+
+        if STOP > 0:
+
+            @pl.when(n < NC - 1)
+            def _():
+                rs_copy(n).start()
+
+        return carry
+
+    lax.fori_loop(0, NC, block, 0)
+    sends = [rs_copy(n) for n in range(NC - 1)] if STOP > 0 else []
     pl.semaphore_wait(met.at[0], 2)
     tell(met.at[1], [line[2], line[NZ - 2]])
     if STOP <= 1:
@@ -140,7 +141,7 @@
         return
     for copy in sends:
         copy.wait_recv()
-    both = ((rsbuf[0] + rsbuf[1]) + (rsbuf[2] + rsbuf[3])).T
+    both = ((part[3] + rsbuf[2]) + (rsbuf[1] + rsbuf[3])).T
     hi, lo = split(both)
     in_hi, in_lo = hi[:RANK], lo[:RANK]
     o_hi, o_lo = hi[RANK:], lo[RANK:]
@@ -206,11 +207,14 @@
     def row_group(xx, count):
         return rowbuf.at[pl.ds(slot(0, xx, k), count)]
 
-    for dx in GROUPS:
-        for dz in (4, 3, 5, 2, 6, 1, 7, 0):
-            if dz or dx:
-                row(dz, dx).start()
-                col(dz, dx).start()
+    def send(t, carry):
+        dx, j = shift(t // NZ), t % NZ
+        dz = NZ // 2 + (1 - 2 * (j % 2)) * ((j + 1) // 2)
+        row(dz, dx).start()
+        col(dz, dx).start()
+        return carry
+
+    lax.fori_loop(0, NZ * NX - 1, send, 0)
     for dx in GROUPS:
         count = NZ if dx else NZ - 1
         xx = (x - dx) % NX
@@ -269,7 +273,7 @@
             pltpu.VMEM((RANK, ff), BF),
             pltpu.VMEM((RANK, d), BF),
             pltpu.VMEM(prior_cov.shape, F32),
-            pltpu.VMEM((3, tok, 2 * RANK), F32),
+            pltpu.VMEM((NC, tok, 2 * RANK), F32),
             pltpu.VMEM((NC, tok, 2 * RANK), F32),
             pltpu.VMEM((RANK, 2 * RANK), F32),
             pltpu.VMEM((NC, RANK // 2, 2 * RANK), F32),
@@ -277,7 +281,7 @@
             pltpu.VMEM((RANK // 2, 2, 2 * RANK), F32),
             pltpu.VMEM((RANK, 2, 2 * RANK), F32),
             pltpu.VMEM((RANK * 16, 2 * RANK), F32),
-            dma((NC, CUTS + 1)),
+            dma((NC, 2)),
             dma((3,)),
             dma((NC,)),
             dma((NC,)),

time: 31.6 us -> 31 us (0.981)
  Pallas kernels: 30.8 us -> 30.2 us
    pallas_call x1, Pallas kernels: 30.8 us -> 30.2 us  [per_device(): pl.pallas_call(kernel, out_shape=pltpu.VMEM(prior_cov.shape, F32), in_spe...]
where the time goes in v3:
time: 31 us; the launch traced here: 30.9 us
  Pallas kernels  30.2 us (97%)
  local copies, waits for them, and re-layouts  0.71 us (2%)
    pallas_call x1, Pallas kernels, per_device(): pl.pallas_call(kernel, out_shape=pltpu.VMEM(prior_cov.shape, F32), in_spe...  30.2 us
    unnamed x1, local copies, waits for them, and re-layouts  0.71 us

profile of v3, /device:TPU:1, one launch (start us, length us, event | category | flops | bytes accessed | tf_op | source)
XLA Modules:
  0.0 30.9 jit_solution(9781884242517647027)
XLA Ops:
  0.0 30.2 %shard_map.55 = f32[64,1024]{1,0:T(8,128)S(1)} custom-call(bf16[512,7168]{1,0:T(8,128)(2,1)} %acts.1, bf16[512,2048]{1,0:T(8,128)(2,1)} %grads.1, bf16[64,7168]{1,0:T(8,128)(2,1)} %bitcast.2, bf16[64,2048]{1,0:T(8,128)(2,1)} %bitcast.3, f32[64,1024]{1,0:T(8,128)} %prior.1), custom_call_target="tpu_custom_call" | custom-call | tf_op jit(solution)/shard_map/pallas_call | solution.py:265
  30.2 0.7 %copy.7 = f32[64,1024]{1,0:T(8,128)} copy(f32[64,1024]{1,0:T(8,128)S(1)} %shard_map.55) | data formatting | bytes 524288

commit v4 on v3

--- a/solution.py
+++ b/solution.py
@@ -32,8 +32,8 @@
 
 def kernel(
     acts, grads, pin, pout, prior, out,
-    a_v, g_v, pi_v, po_v, prior_v, part, rsbuf, tmp, pbuf, sbuf, rowl, rowbuf, colbuf,
-    ld_sem, w_sem, rs_s, rs_r, p_s, p_r, col_s, col_r, row_s, row_r, cc_s, cc_r, cr_s, cr_r, met,
+    a_v, g_v, pi_v, po_v, prior_v, part, rsbuf, tmp, pbuf, sbuf, stage, colbuf,
+    ld_sem, w_sem, rs_s, rs_r, p_s, p_r, col_s, col_r, cc_s, cc_r, met,
 ):
     r = lax.axis_index("seq")
     c = lax.axis_index("tensor")
@@ -147,7 +147,9 @@
     o_hi, o_lo = hi[RANK:], lo[RANK:]
     dup_hi = jnp.concatenate([in_hi, in_hi], axis=0)
     dup_lo = jnp.concatenate([in_lo, in_lo], axis=0)
-    tmp[...] = dot_t(o_hi, dup_hi) + (dot_t(o_hi, dup_lo) + dot_t(o_lo, dup_hi))
+    tmp[...] = dot_t(
+        jnp.concatenate([o_hi, o_hi, o_lo], axis=1), jnp.concatenate([dup_hi, dup_lo, dup_hi], axis=1)
+    )
     half = RANK // 2
     low = lax.broadcasted_iota(jnp.int32, (half, 2 * RANK), 1) < RANK
     pbuf[c] = jnp.where(low, tmp[pl.ds(0, half, stride=2), :], tmp[pl.ds(1, half, stride=2), :])
@@ -167,93 +169,88 @@
     s1 = (pbuf[2] + pbuf[3]) * scale
     sbuf[:half] = s0
     sbuf[half:] = s1
-    rowl[:, 0, :] = s0
-    rowl[:, 1, :] = s1
 
     def slot(zz, xx, kk):
         return (kk * NX + xx) * NZ + zz
 
-    def piece(i):
-        return colbuf.at[pl.ds(pl.multiple_of(i * 16, 16), 16)]
-
     def tile(i):
         return pl.ds(pl.multiple_of(i * 8, 8), 8)
 
     me = slot(z, x, k)
-    own = pl.multiple_of(me * 16, 16)
-    colbuf[pl.ds(own, 8), :] = sbuf[tile(c), :]
-    colbuf[pl.ds(own + 8, 8), :] = sbuf[tile(c + NC), :]
-    rowbuf[me] = rowl[z * NX + x]
+    first, second = sbuf[tile(c), :], sbuf[tile(c + NC), :]
+    for q in range(NZ * NX):
+        stage[q, :8, :] = first
+        stage[q, 8:16, :] = second
+        stage[q, 16:17, :] = s0[q : q + 1]
+        stage[q, 17:18, :] = s1[q : q + 1]
+    colbuf[me, :8, :] = first
+    colbuf[me, 8:16, :] = second
+    colbuf[me, 16:18, :] = stage[z * NX + x, 16:18, :]
     if STOP <= 2:
         for copy in sends + p_copies:
             copy.wait_send()
         prior_copy.wait()
-        out[...] = prior_v[...] + colbuf[0, 0]
+        out[...] = prior_v[...] + colbuf[0, 0, 0]
         return
 
-    def col(dz, dx):
-        peer = (seq_of((z + dz) % NZ, (x + dx) % NX, k), c)
-        return remote(piece(me), piece(me), col_s, col_r.at[dx], peer)
-
-    def row(dz, dx):
+    used = pl.ds(0, 18)
+
+    def message(dz, dx):
         zz, xx = (z + dz) % NZ, (x + dx) % NX
-        return remote(rowl.at[zz * NX + xx], rowbuf.at[me], row_s, row_r.at[dx], (seq_of(zz, xx, k), c))
+        src, dst = stage.at[zz * NX + xx, used], colbuf.at[me, used]
+        return remote(src, dst, col_s, col_r.at[dx], (seq_of(zz, xx, k), c))
 
     sibling = (seq_of(z, x, 1 - k), c)
 
-    def col_group(xx, count):
-        return colbuf.at[pl.ds(pl.multiple_of(slot(0, xx, k) * 16, 128), count * 16)]
-
-    def row_group(xx, count):
-        return rowbuf.at[pl.ds(slot(0, xx, k), count)]
+    def group(xx, count):
+        return colbuf.at[pl.ds(slot(0, xx, k), count), used]
 
     def send(t, carry):
         dx, j = shift(t // NZ), t % NZ
         dz = NZ // 2 + (1 - 2 * (j % 2)) * ((j + 1) // 2)
-        row(dz, dx).start()
-        col(dz, dx).start()
+        message(dz, dx).start()
         return carry
 
     lax.fori_loop(0, NZ * NX - 1, send, 0)
     for dx in GROUPS:
         count = NZ if dx else NZ - 1
         xx = (x - dx) % NX
-        for group, arrival, s, rs in ((col_group, col_r, cc_s, cc_r), (row_group, row_r, cr_s, cr_r)):
-            got = group(xx, count)
-            pltpu.make_async_copy(got, got, arrival.at[dx]).wait()
-            whole = group(xx, NZ)
-            remote(whole, whole, s, rs, sibling).start()
+        got = group(xx, count)
+        pltpu.make_async_copy(got, got, col_r.at[dx]).wait()
+        whole = group(xx, NZ)
+        remote(whole, whole, cc_s, cc_r, sibling).start()
 
     total = NZ * NX
-    mine = colbuf.at[pl.ds(0, total * 16)]
-    mine_rows = rowbuf.at[pl.ds(0, total)]
-    pltpu.make_async_copy(mine_rows, mine_rows, cr_r).wait()
+    mine = colbuf.at[pl.ds(0, total), used]
+    prior_copy.wait()
+    pltpu.make_async_copy(mine, mine, cc_r).wait()
+    flat = colbuf.reshape(RANK * 24, 2 * RANK)
     even = (jnp.zeros((NZ * NX * NK, 2 * RANK), jnp.int32) + k) == 0
     parts = []
     for h in range(2):
-        v = rowbuf[:, h, :]
+        v = flat[pl.ds(16 + h, 64, stride=24), :]
         parts.append(jnp.where(even, v, pltpu.roll(v, RANK, 1)))
     lhs = jnp.concatenate(parts, axis=0).T[:RANK]
     l_hi, l_lo = split(lhs)
-    prior_copy.wait()
-    pltpu.make_async_copy(mine, mine, cc_r).wait()
-    for p in range(8):
+    l_all = jnp.concatenate([l_hi, l_hi, l_lo], axis=1)
+    for p in range(0, 8, 2):
         block = jnp.concatenate(
-            [colbuf[pl.ds(p, 64, stride=16), :], colbuf[pl.ds(8 + p, 64, stride=16), :]], axis=0
+            [
+                jnp.concatenate([flat[pl.ds(8 * h + q, 64, stride=24), :] for h in range(2)], axis=0)
+                for q in (p, p + 1)
+            ],
+            axis=1,
         )
         b_hi, b_lo = split(block)
-        gram = dot(l_hi, b_hi) + (dot(l_hi, b_lo) + dot(l_lo, b_hi))
-        cols = slice(128 * p, 128 * p + 128)
-        out[:, cols] = prior_v[:, cols] + gram * (1.0 / 128.0)
+        product = dot(l_all, jnp.concatenate([b_hi, b_lo, b_hi], axis=0))
+        cols = slice(128 * p, 128 * p + 256)
+        out[:, cols] = prior_v[:, cols] + product * (1.0 / 128.0)
 
     for copy in sends + p_copies:
         copy.wait_send()
-    others = colbuf.at[pl.ds(0, (total - 1) * 16)]
-    other_rows = rowbuf.at[pl.ds(0, total - 1)]
+    others = colbuf.at[pl.ds(0, total - 1), used]
     pltpu.make_async_copy(others, others, col_s).wait()
-    pltpu.make_async_copy(other_rows, other_rows, row_s).wait()
     pltpu.make_async_copy(mine, mine, cc_s).wait()
-    pltpu.make_async_copy(mine_rows, mine_rows, cr_s).wait()
 
 
 def per_device(acts, out_grads, proj_in, proj_out, prior_cov):
@@ -278,9 +275,8 @@
             pltpu.VMEM((RANK, 2 * RANK), F32),
             pltpu.VMEM((NC, RANK // 2, 2 * RANK), F32),
             pltpu.VMEM((RANK, 2 * RANK), F32),
-            pltpu.VMEM((RANK // 2, 2, 2 * RANK), F32),
-            pltpu.VMEM((RANK, 2, 2 * RANK), F32),
-            pltpu.VMEM((RANK * 16, 2 * RANK), F32),
+            pltpu.VMEM((NZ * NX, 24, 2 * RANK), F32),
+            pltpu.VMEM((RANK, 24, 2 * RANK), F32),
             dma((NC, 2)),
             dma((3,)),
             dma((NC,)),
@@ -289,10 +285,6 @@
             dma((NC,)),
             dma(()),
             dma((NX,)),
-            dma(()),
-            dma((NX,)),
-            dma(()),
-            dma(()),
             dma(()),
             dma(()),
             pltpu.SemaphoreType.REGULAR((3,)),

time: 31 us -> 30.8 us (level)
  no operation moved by 1% of the time
where the time goes in v4:
time: 30.8 us; the launch traced here: 30.6 us
  Pallas kernels  29.9 us (97%)
  local copies, waits for them, and re-layouts  0.71 us (2%)
    pallas_call x1, Pallas kernels, per_device(): pl.pallas_call(kernel, out_shape=pltpu.VMEM(prior_cov.shape, F32), in_spe...  29.9 us
    unnamed x1, local copies, waits for them, and re-layouts  0.71 us

profile of v4, /device:TPU:1, one launch (start us, length us, event | category | flops | bytes accessed | tf_op | source)
XLA Modules:
  0.0 30.6 jit_solution(9084284690597787918)
XLA Ops:
  0.0 29.9 %shard_map.55 = f32[64,1024]{1,0:T(8,128)S(1)} custom-call(bf16[512,7168]{1,0:T(8,128)(2,1)} %acts.1, bf16[512,2048]{1,0:T(8,128)(2,1)} %grads.1, bf16[64,7168]{1,0:T(8,128)(2,1)} %bitcast.2, bf16[64,2048]{1,0:T(8,128)(2,1)} %bitcast.3, f32[64,1024]{1,0:T(8,128)} %prior.1), custom_call_target="tpu_custom_call" | custom-call | tf_op jit(solution)/shard_map/pallas_call | solution.py:262
  29.9 0.7 %copy.7 = f32[64,1024]{1,0:T(8,128)} copy(f32[64,1024]{1,0:T(8,128)S(1)} %shard_map.55) | data formatting | bytes 524288

commit v5 on v4

--- a/solution.py
+++ b/solution.py
@@ -63,11 +63,6 @@
     def load_grads(n):
         return pltpu.make_async_copy(grads.at[rows_of(n)], g_v.at[n], ld_sem.at[n, 1])
 
-    weights[0].start()
-    load_acts(0).start()
-    weights[1].start()
-    load_grads(0).start()
-    load_acts(1).start()
 
     barrier = pltpu.get_barrier_semaphore()
     peers = [(r, (c + d) % NC) for d in range(1, NC)]
@@ -81,6 +76,11 @@
             pl.semaphore_signal(sem, inc=1, device_id=peer, device_id_type=MESH)
 
     tell(barrier, peers)
+    weights[0].start()
+    load_acts(0).start()
+    weights[1].start()
+    load_grads(0).start()
+    load_acts(1).start()
 
     def remote(src, dst, s, rs, peer):
         return pltpu.make_async_remote_copy(

time: 30.8 us -> 30.8 us (level)
  no operation moved by 1% of the time
where the time goes in v5:
time: 30.8 us; the launch traced here: 30.6 us
  Pallas kernels  29.9 us (97%)
  local copies, waits for them, and re-layouts  0.71 us (2%)
    pallas_call x1, Pallas kernels, per_device(): pl.pallas_call(kernel, out_shape=pltpu.VMEM(prior_cov.shape, F32), in_spe...  29.9 us
    unnamed x1, local copies, waits for them, and re-layouts  0.71 us

profile of v5, /device:TPU:1, one launch (start us, length us, event | category | flops | bytes accessed | tf_op | source)
XLA Modules:
  0.0 30.6 jit_solution(16514030379445922909)
XLA Ops:
  0.0 29.9 %shard_map.55 = f32[64,1024]{1,0:T(8,128)S(1)} custom-call(bf16[512,7168]{1,0:T(8,128)(2,1)} %acts.1, bf16[512,2048]{1,0:T(8,128)(2,1)} %grads.1, bf16[64,7168]{1,0:T(8,128)(2,1)} %bitcast.2, bf16[64,2048]{1,0:T(8,128)(2,1)} %bitcast.3, f32[64,1024]{1,0:T(8,128)} %prior.1), custom_call_target="tpu_custom_call" | custom-call | tf_op jit(solution)/shard_map/pallas_call | solution.py:262
  29.9 0.7 %copy.7 = f32[64,1024]{1,0:T(8,128)} copy(f32[64,1024]{1,0:T(8,128)S(1)} %shard_map.55) | data formatting | bytes 524288
